TPU v7x, 256 devices: a whole 4x4x8 slice. The times are simulated.
256 devices in a mesh: dp: 4 (over x), expert: 64 (over z, y, core).
Axes of the slice: x: 4, y: 4, z: 8, core: 2. Of those that a mesh axis runs over, the one named last changes fastest.
Arguments:
- tokens: bfloat16 [4096, 3584], P('expert'), may hold values from -6 to 6
- expert_ids: int32 [4096, 8], P('expert'), may hold values from 0 to 63, all different within a row; in each aligned block of 64 rows (0 to 63, 64 to 127, ...) at most 8 rows name the same one
- weight_num: int32 [4096, 8], P('expert'), may hold values from 64 to 1023
- gate_proj: bfloat16 [64, 3584, 2048], P('expert', None, 'dp'), may hold values from -0.09375 to 0.09375
- up_proj: bfloat16 [64, 3584, 2048], P('expert', None, 'dp'), may hold values from -0.09375 to 0.09375
- down_proj: bfloat16 [64, 2048, 3584], P('expert', 'dp'), may hold values from -0.125 to 0.125
Outputs:
- combined: bfloat16 [4096, 3584], P('expert', 'dp')
Inputs may be any that keep to these rules, and one draw needn't show every extreme that they name: `expert_ids`: in the 64 rows of one device no expert is named by more than 8 rows, and some device has an expert named by exactly 8 of its rows.
All inputs are finite; a program needn't handle non-finite values.
Results may differ from a plain program's by a relative error of at most 0.015.
Values may be sent and summed in bfloat16 or wider, within the bound.
A program may use at most 192 MiB of HBM per device.

v0:
```python
import jax
import jax.numpy as jnp
from jax import lax
from jax.sharding import PartitionSpec as P

ROOM = 8


def slot_matrices(ids, num, experts, capacity):
    rows = ids.shape[0]
    slots = experts * capacity
    column = jnp.arange(slots, dtype=jnp.int32)[None, :]
    expert_of = column // capacity
    hits = [ids[:, k : k + 1] == expert_of for k in range(ids.shape[1])]
    named = sum((h.astype(jnp.float32) for h in hits))
    weight = sum((jnp.where(h, num[:, k : k + 1], 0) for k, h in enumerate(hits)))
    earlier = jnp.arange(rows)[:, None] > jnp.arange(rows)[None, :]
    position = jnp.dot(
        earlier.astype(jnp.bfloat16), named.astype(jnp.bfloat16), preferred_element_type=jnp.float32
    )
    here = (named > 0) & (position == (column % capacity).astype(jnp.float32))
    high = jnp.where(here, weight // 32 * 32, 0).astype(jnp.bfloat16)
    low = jnp.where(here, weight % 32, 0).astype(jnp.bfloat16)
    return (here.astype(jnp.bfloat16), high, low)


def local(tokens, expert_ids, weight_num, gate_proj, up_proj, down_proj):
    experts = lax.axis_size("expert")
    parts = lax.axis_size("dp")
    width = tokens.shape[1]
    quarter = width // parts
    slots = experts * ROOM
    here, high, low = slot_matrices(expert_ids, weight_num, experts, ROOM)
    mine = lax.dynamic_slice_in_dim(tokens, lax.axis_index("dp") * quarter, quarter, 1)
    outgoing = lax.dot_general(
        here, mine, (((0,), (0,)), ((), ())), preferred_element_type=jnp.float32
    ).astype(jnp.bfloat16)
    arrived = lax.all_to_all(
        outgoing.reshape(experts, ROOM, quarter), "expert", split_axis=0, concat_axis=0, tiled=True
    ).reshape(slots, quarter)
    rows = lax.all_gather(arrived, "dp", axis=0, tiled=True)
    gate_out, up_out = (0.0, 0.0)
    for q in range(parts):
        block = rows[q * slots : (q + 1) * slots]
        cut = slice(q * quarter, (q + 1) * quarter)
        gate_out += jnp.dot(block, gate_proj[0, cut], preferred_element_type=jnp.float32)
        up_out += jnp.dot(block, up_proj[0, cut], preferred_element_type=jnp.float32)
    hidden = (jax.nn.silu(gate_out) * up_out).astype(jnp.bfloat16)
    partial = jnp.concatenate(
        [
            jnp.dot(
                hidden,
                down_proj[0, :, q * quarter : (q + 1) * quarter],
                preferred_element_type=jnp.float32,
            ).astype(jnp.bfloat16)
            for q in range(parts)
        ],
        axis=0,
    )
    summed = lax.psum_scatter(partial, "dp", scatter_dimension=0, tiled=True)
    returned = lax.all_to_all(
        summed.reshape(experts, ROOM, quarter), "expert", split_axis=0, concat_axis=0, tiled=True
    ).reshape(slots, quarter)
    total = jnp.dot(high, returned, preferred_element_type=jnp.float32)
    total += jnp.dot(low, returned, preferred_element_type=jnp.float32)
    return (total / 1024.0).astype(jnp.bfloat16)


def solution(mesh):
    placed = (
        P("expert", None),
        P("expert", None),
        P("expert", None),
        P("expert", None, "dp"),
        P("expert", None, "dp"),
        P("expert", "dp", None),
    )
    return jax.shard_map(
        local, mesh=mesh, in_specs=placed, out_specs=P("expert", "dp"), check_vma=False
    )
```

profile of v0, /device:TPU:1, one launch (start us, length us, event | category | flops | bytes accessed | tf_op | source)
XLA Modules:
  0.0 203.0 jit_solution(10615380470221626891)
XLA Ops:
  6.5 1.0 slice_bitcast_fusion.15
  7.9 0.5 fusion.1
  8.3 38.4 %all_to_all.10 = bf16[64,8,896]{2,1,0:T(8,128)(2,1)} all-to-all(bf16[64,8,896]{2,1,0:T(8,128)(2,1)S(1)} %fusion.1), channel_id=1, replica_groups=mesh['dp'=4,'expert'=64] {'expert'}, dimensions={0} | all-to-all | bytes 1835008 | tf_op jit(solution)/shard_map/all_to_all | solution.py:38
  46.8 43.6 %all-gather.2.cloned.1.call-done = bf16[2048,896]{1,0:T(8,128)(2,1)} async-done(((bf16[512,896]{1,0:T(8,128)(2,1)}), bf16[2048,896]{1,0:T(8,128)(2,1)}) %all-gather.2.cloned.1.call-update) | async-done | bytes 3670032 | tf_op jit(solution)/shard_map/all_gather | solution.py:41
  90.4 2.3 %fusion.21 = f32[512,512]{1,0:T(8,128)S(1)} fusion(bf16[1,3584,512]{2,1,0:T(8,128)(2,1)} %param.9, bf16[2048,896]{1,0:T(8,128)(2,1)} %all-gather.2.cloned.1.call-done), kind=kOutput, calls=%fused_computation.35 | convolution fusion | flops 469762048 | bytes 2883584 | tf_op jit(solution)/shard_map/dot_general | solution.py:46
  92.7 2.5 %convolution_add_fusion.5 = f32[512,512]{1,0:T(8,128)S(1)} fusion(f32[512,512]{1,0:T(8,128)S(1)} %fusion.21, bf16[1,3584,512]{2,1,0:T(8,128)(2,1)} %param.9, bf16[2048,896]{1,0:T(8,128)(2,1)} %all-gather.2.cloned.1.call-done), kind=kOutput, calls=%fused_computation.12 | convolution fusion | flops 470024192 | bytes 3932160 | tf_op jit(solution)/shard_map/dot_general | solution.py:46
  95.3 0.7 convolution_add_fusion.4
  96.0 0.7 convolution_add_fusion.3
  96.7 0.6 copy-done.3
  97.3 0.7 fusion.16
  98.0 0.7 convolution_add_fusion.2
  98.7 0.7 convolution_add_fusion.1
  99.5 0.8 fusion.2
  100.3 1.2 copy-done.5
  101.5 0.7 convolution_convert_fusion.1
  102.2 0.7 convolution_convert_fusion.2
  102.9 0.7 convolution_convert_fusion.3
  103.7 0.7 convolution_convert_fusion.4
  104.4 8.7 %pad_maximum_fusion = bf16[2048,896]{1,0:T(8,128)(2,1)} fusion(bf16[512,896]{1,0:T(8,128)(2,1)S(1)} %convolution_convert_fusion.1, bf16[512,896]{1,0:T(8,128)(2,1)S(1)} %convolution_convert_fusion.2, bf16[512,896]{1,0:T(8,128)(2,1)S(1)} %convolution_convert_fusion.3, bf16[512,896]{1,0:T(8,128)(2,1)S(1)} %convolution_convert_fusion.4), kind=kLoop, calls=%fused_computation | loop fusion | flops 14680064 | bytes 7340032 | tf_op jit(solution)/shard_map/concatenate | solution.py:49
  113.1 45.6 %reduce-scatter.2.cloned.1.call-done = bf16[512,896]{1,0:T(8,128)(2,1)} async-done(((bf16[2048,896]{1,0:T(8,128)(2,1)}), bf16[512,896]{1,0:T(8,128)(2,1)}) %reduce-scatter.2.cloned.1.call-update) | async-done | bytes 917520 | tf_op jit(solution)/shard_map/reduce_scatter | solution.py:60
  158.7 10.6 %all-to-all-start.1 = ((bf16[64,8,896]{2,1,0:T(8,128)(2,1)}), bf16[64,8,896]{2,1,0:T(8,128)(2,1)S(1)}, u32[]{:S(2)}, u32[]{:S(2)}) async-start(bf16[64,8,896]{2,1,0:T(8,128)(2,1)} %bitcast.83), calls=%async_computation.2 | async-start | bytes 1835008 | tf_op jit(solution)/shard_map/all_to_all | solution.py:61
  169.4 25.3 %all-to-all-done.1 = bf16[64,8,896]{2,1,0:T(8,128)(2,1)S(1)} async-done(((bf16[64,8,896]{2,1,0:T(8,128)(2,1)}), bf16[64,8,896]{2,1,0:T(8,128)(2,1)S(1)}, u32[]{:S(2)}, u32[]{:S(2)}) %all-to-all-start.1) | async-done | bytes 917536 | tf_op jit(solution)/shard_map/all_to_all | solution.py:61
  194.6 0.5 fusion.7
  195.1 1.1 fusion.4
  (17 shorter events, 0.4 us)
Async XLA Ops:
  6.5 1.3 copy-start
  6.5 83.9 %all-gather.2.cloned.1.call-start = ((), (), s32[]{:S(2)}) async-start(), calls=%async_computation.3 | async-start | bytes 4587520 | tf_op jit(solution)/shard_map/all_gather | solution.py:41
  46.7 112.0 %reduce-scatter.2.cloned.1.call-start = ((), (), s32[]{:S(2)}) async-start(), calls=%async_computation.4 | async-start | bytes 4587520 | tf_op jit(solution)/shard_map/reduce_scatter | solution.py:60
  90.4 4.9 %copy-start.1 = (bf16[2048,896]{1,0:T(8,128)(2,1)S(1)}, bf16[2048,896]{1,0:T(8,128)(2,1)}, u32[]{:S(2)}) copy-start(bf16[2048,896]{1,0:T(8,128)(2,1)} %all-gather.2.cloned.1.call-done) | copy-start | bytes 11010052
  90.4 4.9 %copy-start.2 = (bf16[1,3584,512]{2,1,0:T(8,128)(2,1)S(1)}, bf16[1,3584,512]{2,1,0:T(8,128)(2,1)}, u32[]{:S(2)}) copy-start(bf16[1,3584,512]{2,1,0:T(8,128)(2,1)} %param.9) | copy-start | bytes 11010052
  95.3 2.0 %copy-start.3 = (bf16[1,3584,512]{2,1,0:T(8,128)(2,1)S(1)}, bf16[1,3584,512]{2,1,0:T(8,128)(2,1)}, u32[]{:S(2)}) copy-start(bf16[1,3584,512]{2,1,0:T(8,128)(2,1)} %param.10) | copy-start | bytes 11010052
  99.5 2.0 %copy-start.5 = (bf16[1,512,3584]{2,1,0:T(8,128)(2,1)S(1)}, bf16[1,512,3584]{2,1,0:T(8,128)(2,1)}, u32[]{:S(2)}) copy-start(bf16[1,512,3584]{2,1,0:T(8,128)(2,1)} %param.11) | copy-start | bytes 11010052
  113.1 56.2 %copy-start.4 = (s32[64,8]{0,1:T(8,128)S(1)}, s32[64,8]{0,1:T(8,128)}, u32[]{:S(2)}) copy-start(s32[64,8]{0,1:T(8,128)} %param.8) | copy-start | bytes 6148
  158.7 35.9 %all-to-all-start.1 = ((bf16[64,8,896]{2,1,0:T(8,128)(2,1)}), bf16[64,8,896]{2,1,0:T(8,128)(2,1)S(1)}, u32[]{:S(2)}, u32[]{:S(2)}) async-start(bf16[64,8,896]{2,1,0:T(8,128)(2,1)} %bitcast.83), calls=%async_computation.2 | async-start | bytes 1835008 | tf_op jit(solution)/shard_map/all_to_all | solution.py:61
Sparse Core Ops, SparseCore 0:
  46.8 43.5 all-gather.1
  113.2 45.3 reduce-scatter.1
where the time goes:
time: 203 us
  waiting for transfers between devices  115 us (57%)
  blocking collectives  38.4 us (19%)
  matrix products  14.4 us (7%)
  between operations  13.6 us (7%)
  starting transfers between devices  10.7 us (5%)
  other arithmetic  8.73 us (4%)
  local copies, waits for them, and re-layouts  2.81 us (1%)
    reduce_scatter x1, waiting for transfers between devices, local(): summed = lax.psum_scatter(partial, 'dp', scatter_dimension=0, tiled=True)  45.6 us
    all_gather x1, waiting for transfers between devices, local(): rows = lax.all_gather(arrived, 'dp', axis=0, tiled=True)  43.6 us
    all_to_all x1, blocking collectives, local(): lax.all_to_all(outgoing.reshape(experts, ROOM, quarter), 'expert', split_...  38.4 us
    all_to_all x1, waiting for transfers between devices, local(): lax.all_to_all(summed.reshape(experts, ROOM, quarter), 'expert', split_ax...  25.3 us
    all_to_all x1, starting transfers between devices, local(): lax.all_to_all(summed.reshape(experts, ROOM, quarter), 'expert', split_ax...  10.6 us
    concatenate x1, other arithmetic, local(): jnp.concatenate([jnp.dot(hidden, down_proj[0, :, q * quarter:(q + 1) * qu...  8.72 us
    dot_general x4, matrix products, local(): jnp.dot(block, gate_proj[0, cut], preferred_element_type=jnp.float32)  6.26 us
  transfers between devices with their start and end apart: 3, of which 3 were waited for; matrix products, arithmetic and copies ran while one was open for 0% of the time, Pallas kernels for 0%

commit v1 on v0

--- a/solution.py
+++ b/solution.py
@@ -4,6 +4,24 @@
 from jax.sharding import PartitionSpec as P
 
 ROOM = 8
+
+
+def gather_around(value, axis, dim):
+    ways, here, hop = (lax.axis_size(axis), lax.axis_index(axis), value.shape[dim])
+    dims = [n * ways if d == dim else n for d, n in enumerate(value.shape)]
+    full = lax.dynamic_update_slice_in_dim(
+        jnp.zeros(dims, value.dtype), value, here * hop, axis=dim
+    )
+    going_up = going_down = value
+    for far in range(1, ways // 2 + 1):
+        going_up = lax.ppermute(going_up, axis, [(d, (d + 1) % ways) for d in range(ways)])
+        full = lax.dynamic_update_slice_in_dim(full, going_up, (here - far) % ways * hop, axis=dim)
+        if 2 * far < ways:
+            going_down = lax.ppermute(going_down, axis, [(d, (d - 1) % ways) for d in range(ways)])
+            full = lax.dynamic_update_slice_in_dim(
+                full, going_down, (here + far) % ways * hop, axis=dim
+            )
+    return full
 
 
 def slot_matrices(ids, num, experts, capacity):
@@ -38,7 +56,7 @@
     arrived = lax.all_to_all(
         outgoing.reshape(experts, ROOM, quarter), "expert", split_axis=0, concat_axis=0, tiled=True
     ).reshape(slots, quarter)
-    rows = lax.all_gather(arrived, "dp", axis=0, tiled=True)
+    rows = gather_around(arrived, "dp", 0)
     gate_out, up_out = (0.0, 0.0)
     for q in range(parts):
         block = rows[q * slots : (q + 1) * slots]

time: 203 us -> 196 us (0.966)
  waiting for transfers between devices: 115 us -> 106 us
  matrix products: 14.4 us -> 11 us
  starting transfers between devices: 10.7 us -> 13.4 us
  local copies, waits for them, and re-layouts: 2.81 us -> 4.88 us
    all_gather x1 -> x0, waiting for transfers between devices: 43.6 us -> none  [local(): rows = lax.all_gather(arrived, 'dp', axis=0, tiled=True)]
    ppermute x0 -> x3, waiting for transfers between devices: none -> 37.9 us  [the longest x2 37.9 us: gather_around(): lax.ppermute(going_up, axis, [(d, (d + 1) % ways) for d in range(ways)])]
    dot_general x4, matrix products: 6.26 us -> 2.83 us  [local(): jnp.dot(block, gate_proj[0, cut], preferred_element_type=jnp.float32)]
    ppermute x0 -> x3, starting transfers between devices: none -> 2.78 us  [the longest x1 1.47 us: gather_around(): lax.ppermute(going_down, axis, [(d, (d - 1) % ways) for d in range(ways)])]
    reduce_scatter x1, waiting for transfers between devices: 45.6 us -> 43.2 us  [local(): summed = lax.psum_scatter(partial, 'dp', scatter_dimension=0, tiled=True)]
  transfers between devices with their start and end apart: 3 -> 5, of which waited for: 3 -> 4; matrix products, arithmetic and copies ran while one was open for 0% -> 1% of each run, Pallas kernels for 0% -> 0%
where the time goes in v1:
time: 196 us
  waiting for transfers between devices  106 us (54%)
  blocking collectives  38.3 us (20%)
  between operations  13.6 us (7%)
  starting transfers between devices  13.4 us (7%)
  matrix products  11 us (6%)
  other arithmetic  8.73 us (4%)
  local copies, waits for them, and re-layouts  4.88 us (2%)
    reduce_scatter x1, waiting for transfers between devices, local(): summed = lax.psum_scatter(partial, 'dp', scatter_dimension=0, tiled=True)  43.2 us
    all_to_all x1, blocking collectives, local(): lax.all_to_all(outgoing.reshape(experts, ROOM, quarter), 'expert', split_...  38.3 us
    ppermute x2, waiting for transfers between devices, gather_around(): lax.ppermute(going_up, axis, [(d, (d + 1) % ways) for d in range(ways)])  37.9 us
    all_to_all x1, waiting for transfers between devices, local(): lax.all_to_all(summed.reshape(experts, ROOM, quarter), 'expert', split_ax...  25.3 us
    all_to_all x1, starting transfers between devices, local(): lax.all_to_all(summed.reshape(experts, ROOM, quarter), 'expert', split_ax...  10.6 us
    concatenate x1, other arithmetic, local(): jnp.concatenate([jnp.dot(hidden, down_proj[0, :, q * quarter:(q + 1) * qu...  8.73 us
  transfers between devices with their start and end apart: 5, of which 4 were waited for; matrix products, arithmetic and copies ran while one was open for 1% of the time, Pallas kernels for 0%

profile of v1, /device:TPU:1, one launch (start us, length us, event | category | flops | bytes accessed | tf_op | source)
XLA Modules:
  0.0 196.2 jit_solution(454965008988232089)
XLA Ops:
  6.5 1.0 slice_bitcast_fusion.15
  8.3 38.3 %all_to_all.10 = bf16[64,8,896]{2,1,0:T(8,128)(2,1)S(1)} all-to-all(bf16[64,8,896]{2,1,0:T(8,128)(2,1)S(1)} %fusion.4), channel_id=1, replica_groups=mesh['dp'=4,'expert'=64] {'expert'}, dimensions={0} | all-to-all | bytes 1835008 | tf_op jit(solution)/shard_map/all_to_all | solution.py:56
  46.6 1.2 collective-permute-start
  47.8 1.5 collective-permute-start.1
  49.3 19.1 %collective-permute-done = bf16[512,896]{1,0:T(8,128)(2,1)S(1)} collective-permute-done((bf16[512,896]{1,0:T(8,128)(2,1)S(1)}, bf16[512,896]{1,0:T(8,128)(2,1)S(1)}, u32[]{:S(2)}, u32[]{:S(2)}) %collective-permute-start) | collective-permute-done | bytes 917536 | tf_op jit(solution)/shard_map/ppermute | solution.py:17
  69.1 1.5 constant_dynamic-update-slice_fusion.1
  70.6 18.7 %collective-permute-done.2 = bf16[512,896]{1,0:T(8,128)(2,1)S(1)} collective-permute-done((bf16[512,896]{1,0:T(8,128)(2,1)S(1)}, bf16[512,896]{1,0:T(8,128)(2,1)S(1)}, u32[]{:S(2)}, u32[]{:S(2)}) %collective-permute-start.2) | collective-permute-done | bytes 917536 | tf_op jit(solution)/shard_map/ppermute | solution.py:17
  89.4 0.7 fusion.24
  90.2 0.7 fusion.26
  90.9 0.7 fusion.28
  92.9 0.7 fusion.17
  93.6 0.7 fusion.19
  94.3 0.7 fusion.3
  95.0 0.9 multiply_convert_fusion
  96.0 1.1 copy-done.4
  97.1 0.7 convolution_convert_fusion.1
  97.8 0.7 convolution_convert_fusion.2
  98.5 0.7 convolution_convert_fusion.3
  99.2 0.7 convolution_convert_fusion.4
  99.9 8.7 %pad_maximum_fusion = bf16[2048,896]{1,0:T(8,128)(2,1)} fusion(bf16[512,896]{1,0:T(8,128)(2,1)S(1)} %convolution_convert_fusion.1, bf16[512,896]{1,0:T(8,128)(2,1)S(1)} %convolution_convert_fusion.2, bf16[512,896]{1,0:T(8,128)(2,1)S(1)} %convolution_convert_fusion.3, bf16[512,896]{1,0:T(8,128)(2,1)S(1)} %convolution_convert_fusion.4), kind=kLoop, calls=%fused_computation | loop fusion | flops 14680064 | bytes 7340032 | tf_op jit(solution)/shard_map/concatenate | solution.py:67
  108.7 43.2 %reduce-scatter.2.cloned.1.call-done = bf16[512,896]{1,0:T(8,128)(2,1)} async-done(((bf16[2048,896]{1,0:T(8,128)(2,1)}), bf16[512,896]{1,0:T(8,128)(2,1)}) %reduce-scatter.2.cloned.1.call-update) | async-done | bytes 917520 | tf_op jit(solution)/shard_map/reduce_scatter | solution.py:78
  151.8 10.6 %all-to-all-start.1 = ((bf16[64,8,896]{2,1,0:T(8,128)(2,1)}), bf16[64,8,896]{2,1,0:T(8,128)(2,1)S(1)}, u32[]{:S(2)}, u32[]{:S(2)}) async-start(bf16[64,8,896]{2,1,0:T(8,128)(2,1)} %bitcast.87), calls=%async_computation.2 | async-start | bytes 1835008 | tf_op jit(solution)/shard_map/all_to_all | solution.py:79
  162.5 25.3 %all-to-all-done.1 = bf16[64,8,896]{2,1,0:T(8,128)(2,1)S(1)} async-done(((bf16[64,8,896]{2,1,0:T(8,128)(2,1)}), bf16[64,8,896]{2,1,0:T(8,128)(2,1)S(1)}, u32[]{:S(2)}, u32[]{:S(2)}) %all-to-all-start.1) | async-done | bytes 917536 | tf_op jit(solution)/shard_map/all_to_all | solution.py:79
  188.2 1.1 fusion.6
  (23 shorter events, 3.4 us)
Async XLA Ops:
  6.5 1.3 copy-start
  6.5 145.3 %reduce-scatter.2.cloned.1.call-start = ((), (), s32[]{:S(2)}) async-start(), calls=%async_computation.3 | async-start | bytes 4587520 | tf_op jit(solution)/shard_map/reduce_scatter | solution.py:78
  46.6 21.8 %collective-permute-start = (bf16[512,896]{1,0:T(8,128)(2,1)S(1)}, bf16[512,896]{1,0:T(8,128)(2,1)S(1)}, u32[]{:S(2)}, u32[]{:S(2)}) collective-permute-start(bf16[512,896]{1,0:T(8,128)(2,1)S(1)} %bitcast.85), channel_id=1, source_target_pairs={{0,64},{64,128},{128,192},{192,0},{1,65},{65,129},{129,193},{193,1... | collective-permute-start | bytes 2752520 | tf_op jit(solution)/shard_map/ppermute | solution.py:17
  47.8 21.3 %collective-permute-start.1 = (bf16[512,896]{1,0:T(8,128)(2,1)S(1)}, bf16[512,896]{1,0:T(8,128)(2,1)}, u32[]{:S(2)}, u32[]{:S(2)}) collective-permute-start(bf16[512,896]{1,0:T(8,128)(2,1)S(1)} %bitcast.86), channel_id=1, source_target_pairs={{0,192},{64,0},{128,64},{192,128},{1,193},{65,1},{129,65},{193,129... | collective-permute-start | bytes 2752520 | tf_op jit(solution)/shard_map/ppermute | solution.py:20
  68.4 20.9 %collective-permute-start.2 = (bf16[512,896]{1,0:T(8,128)(2,1)S(1)}, bf16[512,896]{1,0:T(8,128)(2,1)S(1)}, u32[]{:S(2)}, u32[]{:S(2)}) collective-permute-start(bf16[512,896]{1,0:T(8,128)(2,1)S(1)} %collective-permute-done), channel_id=1, source_target_pairs={{0,64},{64,128},{128,192},{192,0},{1,65},{65,129},{129,193},{193,1... | collective-permute-start | bytes 2752520 | tf_op jit(solution)/shard_map/ppermute | solution.py:17
  68.8 20.6 %copy-start.1 = (bf16[1,3584,512]{2,1,0:T(8,128)(2,1)S(1)}, bf16[1,3584,512]{2,1,0:T(8,128)(2,1)}, u32[]{:S(2)}) copy-start(bf16[1,3584,512]{2,1,0:T(8,128)(2,1)} %param.9) | copy-start | bytes 11010052
  90.1 2.0 %copy-start.3 = (bf16[1,3584,512]{2,1,0:T(8,128)(2,1)S(1)}, bf16[1,3584,512]{2,1,0:T(8,128)(2,1)}, u32[]{:S(2)}) copy-start(bf16[1,3584,512]{2,1,0:T(8,128)(2,1)} %param.10) | copy-start | bytes 11010052
  95.0 2.0 %copy-start.4 = (bf16[1,512,3584]{2,1,0:T(8,128)(2,1)S(1)}, bf16[1,512,3584]{2,1,0:T(8,128)(2,1)}, u32[]{:S(2)}) copy-start(bf16[1,512,3584]{2,1,0:T(8,128)(2,1)} %param.11) | copy-start | bytes 11010052
  108.7 53.8 %copy-start.2 = (s32[64,8]{0,1:T(8,128)S(1)}, s32[64,8]{0,1:T(8,128)}, u32[]{:S(2)}) copy-start(s32[64,8]{0,1:T(8,128)} %param.8) | copy-start | bytes 6148
  151.8 35.9 %all-to-all-start.1 = ((bf16[64,8,896]{2,1,0:T(8,128)(2,1)}), bf16[64,8,896]{2,1,0:T(8,128)(2,1)S(1)}, u32[]{:S(2)}, u32[]{:S(2)}) async-start(bf16[64,8,896]{2,1,0:T(8,128)(2,1)} %bitcast.87), calls=%async_computation.2 | async-start | bytes 1835008 | tf_op jit(solution)/shard_map/all_to_all | solution.py:79
Sparse Core Ops, SparseCore 0:
  108.8 42.9 reduce-scatter.1
